TPU v7x, 32 devices: a whole 2x2x4 slice. The times are simulated.
32 devices in a mesh: tm: 16 (over z, y, x), mp: 2 (over core).
Axes of the slice: x: 2, y: 2, z: 4, core: 2. Of those that a mesh axis runs over, the one named last changes fastest.
Arguments:
- filterbank: bfloat16 [4, 16384, 80], P(None, 'tm'), may hold values from -6 to 6
- lengths: int32 [4], replicated, may hold values from 2048 to 4096, as said below
- bank_begin: int32 [4, 1024], P(None, 'tm'), may hold values from 0 to 1023, as said below
- memory_in: bfloat16 [4, 1024, 1024], P(None, 'tm', 'mp'), may hold values from -6 to 6
- w_front: bfloat16 [320, 1024], P(None, 'mp'), may hold values from -0.3125 to 0.3125
- gain_attn: float32 [1024], replicated, may hold values from 0.25 to 1.75
- w_query: bfloat16 [1024, 1024], P(None, 'mp'), may hold values from -0.1875 to 0.1875
- w_key: bfloat16 [1024, 1024], P(None, 'mp'), may hold values from -0.1875 to 0.1875
- w_value: bfloat16 [1024, 1024], P(None, 'mp'), may hold values from -0.1875 to 0.1875
- w_out: bfloat16 [1024, 1024], P('mp'), may hold values from -0.1875 to 0.1875
- gain_ffn: float32 [1024], replicated, may hold values from 0.25 to 1.75
- w_up: bfloat16 [1024, 4096], P(None, 'mp'), may hold values from -0.1875 to 0.1875
- w_down: bfloat16 [4096, 1024], P('mp'), may hold values from -0.09375 to 0.09375
Outputs:
- encoded: bfloat16 [4, 4096, 1024], P(None, 'tm', 'mp')
- memory_out: bfloat16 [4, 1024, 1024], P(None, 'tm', 'mp')
Inputs may be any that keep to these rules, and one draw needn't show every extreme that they name: `lengths`: some utterance has all 4096 frames. For segment i: max(0, i - 32) <= bank_begin <= max(0, i - 16); in each utterance some segment has bank_begin = i - 32.
All inputs are finite; a program needn't handle non-finite values.
Results may differ from a plain program's by a relative error of at most 0.012.
Values may be sent and summed in bfloat16 or wider, within the bound.
A program may use at most 128 MiB of HBM per device.

v0:
```python
import jax
import jax.numpy as jnp
from jax import lax
from jax.sharding import PartitionSpec as P

HEAD_DIM = 64
STACK = 4
SEG = 4
LC = 32
RC = 4
M = 32
epsilon = 1e-05


def from_behind(block, axis, distance):
    devices = range(lax.axis_size(axis))
    route = [(i - distance, i) for i in devices if i - distance in devices]
    return lax.ppermute(block, axis, route)


def normalize(values, gain):
    center = jnp.mean(values, axis=-1, keepdims=True)
    shifted = values - center
    spread = jnp.mean(shifted * shifted, axis=-1, keepdims=True)
    return shifted * lax.rsqrt(spread + epsilon) * gain


def product(inputs, weight):
    flat_rows = inputs.reshape(-1, inputs.shape[-1])
    result = jnp.dot(flat_rows, weight, preferred_element_type=jnp.float32)
    return result.reshape(inputs.shape[:-1] + (weight.shape[1],))


def rounded(values):
    return lax.optimization_barrier(values.astype(jnp.bfloat16)).astype(jnp.float32)


def body(
    filterbank,
    lengths,
    bank_begin,
    memory_in,
    w_front,
    gain_attn,
    w_query,
    w_key,
    w_value,
    w_out,
    gain_ffn,
    w_up,
    w_down,
):
    batch_count = filterbank.shape[0]
    frames_dev = filterbank.shape[1] // STACK
    segs_dev = frames_dev // SEG
    full_width = w_query.shape[0]
    part_width = w_query.shape[1]
    head_count = part_width // HEAD_DIM
    half_width = full_width // lax.axis_size("mp")
    device_index = lax.axis_index("tm")
    model_index = lax.axis_index("mp")
    column_start = model_index * half_width
    first_frame = device_index * frames_dev
    frame_pos = first_frame + jnp.arange(frames_dev, dtype=jnp.int32)
    valid_frame = frame_pos[None, :] < lengths[:, None]
    seg_global = device_index * segs_dev + jnp.arange(segs_dev, dtype=jnp.int32)
    valid_seg = seg_global[None, :] * SEG < lengths[:, None]
    stacked = filterbank.reshape(batch_count, frames_dev, STACK * filterbank.shape[2])
    front_half = jnp.where(valid_frame[:, :, None], product(stacked, w_front), 0.0).astype(
        jnp.bfloat16
    )
    inputs, memory_full = (
        lax.all_gather(front_half, "mp", axis=2, tiled=True),
        lax.all_gather(memory_in, "mp", axis=2, tiled=True),
    )
    inputs_f = inputs.astype(jnp.float32)
    summary = jnp.mean(inputs_f.reshape(batch_count, segs_dev, SEG, full_width), axis=2)
    normed_all = jnp.concatenate(
        [
            normalize(inputs_f, gain_attn),
            normalize(summary, gain_attn),
            normalize(memory_full.astype(jnp.float32), gain_attn),
        ],
        axis=1,
    ).astype(jnp.bfloat16)
    query_rows = product(normed_all[:, : frames_dev + segs_dev], w_query).astype(jnp.bfloat16)
    key_input = jnp.concatenate(
        [normed_all[:, :frames_dev], normed_all[:, frames_dev + segs_dev :]], axis=1
    )
    key_rows = product(key_input, w_key).astype(jnp.bfloat16)
    value_rows = product(key_input, w_value).astype(jnp.bfloat16)
    frame_keys = key_rows[:, :frames_dev]
    frame_values = value_rows[:, :frames_dev]
    bank_pair = jnp.stack([key_rows[:, frames_dev:], value_rows[:, frames_dev:]])
    left_pair = from_behind(
        jnp.stack([frame_keys[:, frames_dev - LC :], frame_values[:, frames_dev - LC :]]), "tm", 1
    )
    right_pair = from_behind(jnp.stack([frame_keys[:, :RC], frame_values[:, :RC]]), "tm", -1)
    hop_count = -(-M // segs_dev)
    gathered = []
    moving = bank_pair
    moving = from_behind(moving, "tm", 1)
    gathered.insert(0, moving)
    bank_all = jnp.concatenate(gathered + [bank_pair], axis=2)
    all_keys = jnp.concatenate([left_pair[0], frame_keys, right_pair[0], bank_all[0]], axis=1)
    all_values = jnp.concatenate([left_pair[1], frame_values, right_pair[1], bank_all[1]], axis=1)
    query_count = frames_dev + segs_dev
    local_seg = jnp.concatenate(
        [jnp.arange(frames_dev, dtype=jnp.int32) // SEG, jnp.arange(segs_dev, dtype=jnp.int32)]
    )
    query_seg = device_index * segs_dev + local_seg
    bank_floor = jnp.concatenate([jnp.repeat(bank_begin, SEG, axis=1), bank_begin], axis=1)
    key_pos = first_frame - LC + jnp.arange(LC + frames_dev + RC, dtype=jnp.int32)
    key_grid = key_pos[None, None, :]
    seg_grid = query_seg[None, :, None]
    frame_allowed = (
        (key_grid >= seg_grid * SEG - LC)
        & (key_grid < (seg_grid + 1) * SEG + RC)
        & (key_grid >= 0)
        & (key_grid < lengths[:, None, None])
    )
    bank_seg = (device_index - hop_count) * segs_dev + jnp.arange(
        (hop_count + 1) * segs_dev, dtype=jnp.int32
    )
    bank_grid = bank_seg[None, None, :]
    bank_allowed = (bank_grid >= bank_floor[:, :, None]) & (bank_grid <= seg_grid - 1)
    allowed = jnp.concatenate([frame_allowed, bank_allowed], axis=2)
    query_heads = query_rows.reshape(batch_count, query_count, head_count, HEAD_DIM)
    key_heads = all_keys.reshape(batch_count, -1, head_count, HEAD_DIM)
    value_heads = all_values.reshape(batch_count, -1, head_count, HEAD_DIM)
    scores = jnp.einsum(
        "bqhd,bkhd->bhqk", query_heads, key_heads, preferred_element_type=jnp.float32
    ) * HEAD_DIM ** (-0.5)
    weights = jnp.where(allowed[:, None], jnp.exp(scores), 0.0)
    shares = (weights / jnp.sum(weights, axis=-1, keepdims=True)).astype(jnp.bfloat16)
    context = jnp.einsum("bhqk,bkhd->bqhd", shares, value_heads, preferred_element_type=jnp.float32)
    context = context.astype(jnp.bfloat16).reshape(batch_count, query_count, part_width)
    mixed_term = rounded(product(context, w_out))
    frame_term = mixed_term[:, :frames_dev]
    summary_term = mixed_term[:, frames_dev:]
    attention, memory_half = (
        lax.psum_scatter(
            frame_term.astype(jnp.bfloat16), "mp", scatter_dimension=2, tiled=True
        ).astype(jnp.float32),
        lax.psum_scatter(
            summary_term.astype(jnp.bfloat16), "mp", scatter_dimension=2, tiled=True
        ).astype(jnp.float32),
    )
    residual = (front_half.astype(jnp.float32) + attention).astype(jnp.bfloat16)
    residual_f = residual.astype(jnp.float32)
    first_moment, second_moment = lax.psum(
        (jnp.sum(residual_f, axis=-1), jnp.sum(residual_f * residual_f, axis=-1)), "mp"
    )
    center = first_moment / full_width
    spread = second_moment / full_width - center * center
    gain_half = lax.dynamic_slice_in_dim(gain_ffn, column_start, half_width, 0)
    normed_half = (
        (residual_f - center[..., None]) * lax.rsqrt(spread[..., None] + epsilon) * gain_half
    ).astype(jnp.bfloat16)
    normed_ffn = lax.all_gather(normed_half, "mp", axis=2, tiled=True)
    hidden = jax.nn.gelu(product(normed_ffn, w_up)).astype(jnp.bfloat16)
    feed_half = lax.psum_scatter(
        rounded(product(hidden, w_down)).astype(jnp.bfloat16), "mp", scatter_dimension=2, tiled=True
    ).astype(jnp.float32)
    encoded = jnp.where(
        valid_frame[:, :, None], residual.astype(jnp.float32) + feed_half, 0.0
    ).astype(jnp.bfloat16)
    memory_out = jnp.where(valid_seg[:, :, None], memory_half, 0.0).astype(jnp.bfloat16)
    return (encoded, memory_out)


def solution(mesh):
    in_specs = (
        P(None, "tm", None),
        P(),
        P(None, "tm"),
        P(None, "tm", "mp"),
        P(None, "mp"),
        P(),
        P(None, "mp"),
        P(None, "mp"),
        P(None, "mp"),
        P("mp", None),
        P(),
        P(None, "mp"),
        P("mp", None),
    )
    out_specs = (P(None, "tm", "mp"), P(None, "tm", "mp"))
    return jax.shard_map(body, mesh=mesh, in_specs=in_specs, out_specs=out_specs, check_vma=False)
```

profile of v0, /device:TPU:0, one launch (start us, length us, event | category | flops | bytes accessed | tf_op | source)
XLA Modules:
  0.0 166.0 jit_solution(9979901539850414377)
XLA Ops:
  7.3 1.6 copy.25
  9.7 2.6 %select_convert_fusion = bf16[4,256,512]{2,1,0:T(8,128)(2,1)} fusion(bf16[4,256,320]{2,1,0:T(8,128)(2,1)S(1)} %dot_general.31, pred[4,256]{1,0:T(4,128)(4,1)S(1)} %broadcast_compare_fusion.2, bf16[320,512]{1,0:T(8,128)(2,1)} %param.17), kind=kOutput, calls=%fused_computation.55 | convolution fusion | flops 336592896 | bytes 2032640 | tf_op jit(solution)/shard_map/dot_general | solution.py:30
  12.4 2.3 %all_gather.10 = bf16[4,64,1024]{2,1,0:T(8,128)(2,1)S(1)} all-gather(bf16[4,64,512]{2,1,0:T(8,128)(2,1)S(1)} %copy-done.18), channel_id=1, replica_groups=mesh['tm'=16,'mp'=2] {'mp'}, dimensions={2}, use_global_device_ids=true | all-gather | bytes 786432 | tf_op jit(solution)/shard_map/all_gather | solution.py:74
  17.5 8.4 %all-gather.3.cloned.1.call-done = bf16[4,256,1024]{2,1,0:T(8,128)(2,1)} async-done(((bf16[4,256,512]{2,1,0:T(8,128)(2,1)}), bf16[4,256,1024]{2,1,0:T(8,128)(2,1)}) %all-gather.3.cloned.1.call-update) | async-done | bytes 2097168 | tf_op jit(solution)/shard_map/all_gather | solution.py:73
  25.8 4.8 %reshape.352 = f32[4,64,4,1024]{3,2,1,0:T(4,128)} reshape(bf16[4,256,1024]{2,1,0:T(8,128)(2,1)} %all-gather.3.cloned.1.call-done) | data formatting | bytes 6291456 | tf_op jit(solution)/shard_map/reshape | solution.py:77
  30.6 5.9 %reduce_sum.94 = f32[4,64,1024]{2,1,0:T(8,128)} reduce(f32[4,64,4,1024]{3,2,1,0:T(4,128)} %reshape.352, f32[]{:T(128)} %constant.29.clone.1), dimensions={2}, to_apply=%region_4.5 | reduce | flops 786432 | bytes 5242884 | tf_op jit(solution)/shard_map/reduce_sum | solution.py:77
  37.9 1.6 multiply_reduce_fusion.1
  43.8 1.5 fusion.60
  46.3 4.5 %collective-permute-start = (bf16[2,4,32,512]{3,2,1,0:T(8,128)(2,1)}, bf16[2,4,32,512]{3,2,1,0:T(8,128)(2,1)}, u32[]{:S(2)}, u32[]{:S(2)}) collective-permute-start(bf16[2,4,32,512]{3,2,1,0:T(8,128)(2,1)} %pad_maximum_fusion.8), channel_id=1, source_target_pairs={{0,2},{2,4},{4,6},{6,8},{8,10},{10,12},{12,14},{14,16},{16,18},{18... | collective-permute-start | bytes 786440 | tf_op jit(solution)/shard_map/ppermute | solution.py:18
  52.9 5.3 %collective-permute-start.2 = (bf16[2,4,64,512]{3,2,1,0:T(8,128)(2,1)}, bf16[2,4,64,512]{3,2,1,0:T(8,128)(2,1)}, u32[]{:S(2)}, u32[]{:S(2)}) collective-permute-start(bf16[2,4,64,512]{3,2,1,0:T(8,128)(2,1)} %pad_maximum_fusion.7), channel_id=1, source_target_pairs={{0,2},{2,4},{4,6},{6,8},{8,10},{10,12},{12,14},{14,16},{16,18},{18... | collective-permute-start | bytes 1572872 | tf_op jit(solution)/shard_map/ppermute | solution.py:18
  58.3 2.6 %fusion.61 = bf16[4,320,512]{2,1,0:T(8,128)(2,1)} fusion(bf16[4,64,1024]{2,1,0:T(8,128)(2,1)S(1)} %get-tuple-element.16, bf16[4,256,1024]{2,1,0:T(8,128)(2,1)S(1)} %multiply_convert_fusion, bf16[1024,512]{1,0:T(8,128)(2,1)S(1)} %copy-done.25), kind=kOutput, calls=%fused_computation.63 | convolution fusion | flops 1348075520 | bytes 4980736 | tf_op jit(solution)/shard_map/dot_general | solution.py:30
  63.4 2.6 %copy.31 = bf16[4,320,512]{1,2,0:T(8,128)(2,1)} copy(bf16[4,320,512]{2,1,0:T(8,128)(2,1)} %fusion.61) | data formatting | bytes 2621440 | tf_op jit(solution)/shard_map/convert_element_type | solution.py:86
  75.2 12.9 %fusion = (f32[4,8,320]{2,1,0:T(8,128)S(1)}, f32[4,8,320,420]{2,3,1,0:T(8,128)}) fusion(pred[4,320,420]{1,2,0:T(8,128)(4,1)} %pad_add_fusion, bf16[4,320,8,64]{1,3,2,0:T(8,128)(2,1)} %bitcast.57, bf16[4,128,8,64]{1,3,2,0:T(8,128)(2,1)} %bitcast.65, bf16[4,4,8,64]{1,3,2,0:T(8,128)(2,1)} %bitcast.63, bf16[4,256,8,64]{1,3,2,0:T(8,128)(2,1)S(1)} %bitcast.59, ...), kind=kOutput, calls=%fused_computation.2 | convolution fusion | flops 570275840 | bytes 20812800 | tf_op jit(solution)/shard_map/bqhd,bkhd->bhqk/dot_general | solution.py:131
  88.1 10.9 %fusion.54 = bf16[4,8,64,320]{3,2,1,0:T(8,128)(2,1)S(1)} fusion(f32[4,8,320,420]{2,3,1,0:T(8,128)} %get-tuple-element.21, f32[4,8,320]{2,1,0:T(8,128)S(1)} %get-tuple-element.20, pred[4,320,420]{1,2,0:T(8,128)(4,1)S(1)} %copy-done.15, bf16[4,128,8,64]{1,3,2,0:T(8,128)(2,1)S(1)} %bitcast.64, bf16[4,4,8,64]{1,3,2,0:T(8,128)(2,1)S(1)} %bitcast.62, ...), kind=kOutput, calls=%fused_computation.58 | convolution fusion | flops 575242240 | bytes 20812800 | tf_op jit(solution)/shard_map/bhqk,bkhd->bqhd/dot_general | solution.py:136
  99.1 1.6 convolution_convert_fusion
  104.0 9.9 %reduce-scatter.4.cloned.1.call-done = bf16[4,256,512]{2,1,0:T(8,128)(2,1)} async-done(((bf16[4,256,1024]{2,1,0:T(8,128)(2,1)}), bf16[4,256,512]{2,1,0:T(8,128)(2,1)}) %reduce-scatter.4.cloned.1.call-update) | async-done | bytes 1048592 | tf_op jit(solution)/shard_map/reduce_scatter | solution.py:142
  113.9 1.8 %convert_reduce_fusion = (f32[4,256]{1,0:T(4,128)S(1)}, f32[4,256]{1,0:T(4,128)S(1)}, bf16[4,256,512]{2,1,0:T(8,128)(2,1)S(1)}) fusion(bf16[4,256,512]{2,1,0:T(8,128)(2,1)} %reduce-scatter.4.cloned.1.call-done, bf16[4,256,512]{2,1,0:T(8,128)(2,1)S(1)} %copy-done.5), kind=kLoop, calls=%fused_computation.25 | loop fusion | flops 4192256 | bytes 3153920 | tf_op jit(solution)/shard_map/reduce_sum | solution.py:152
  115.7 2.5 %all-reduce = (f32[4,256]{1,0:T(4,128)S(1)}, f32[4,256]{1,0:T(4,128)S(1)}) all-reduce(f32[4,256]{1,0:T(4,128)S(1)} %get-tuple-element.3, f32[4,256]{1,0:T(4,128)S(1)} %get-tuple-element.2), channel_id=1, replica_groups=mesh['tm'=16,'mp'=2] {'mp'}, use_global_device_ids=true, to_apply=%region_12.13 | all-reduce | flops 2048 | bytes 16384 | tf_op jit(solution)/shard_map/psum | solution.py:151
  119.7 1.9 %slice.95 = bf16[4,64,1024]{2,1,0:T(8,128)(2,1)} slice(bf16[4,320,1024]{2,1,0:T(8,128)(2,1)} %copy-done.8), slice={[0:4], [256:320], [0:1024]} | slice | bytes 1048576 | tf_op jit(solution)/shard_map/slice | solution.py:140
  121.6 10.0 %all-gather.5.cloned.1.call-done = bf16[4,256,1024]{2,1,0:T(8,128)(2,1)} async-done(((bf16[4,256,512]{2,1,0:T(8,128)(2,1)}), bf16[4,256,1024]{2,1,0:T(8,128)(2,1)}) %all-gather.5.cloned.1.call-update) | async-done | bytes 2097168 | tf_op jit(solution)/shard_map/all_gather | solution.py:160
  131.6 14.3 %fusion.47 = bf16[4,256,1024]{2,1,0:T(8,128)(2,1)} fusion(bf16[2048,1024]{1,0:T(8,128)(2,1)} %param.25, bf16[4,256,1024]{2,1,0:T(8,128)(2,1)} %all-gather.5.cloned.1.call-done, bf16[1024,2048]{1,0:T(8,128)(2,1)} %param.24), kind=kOutput, calls=%fused_computation.57 | convolution fusion | flops 8609857536 | bytes 12582912 | tf_op jit(solution)/shard_map/dot_general | solution.py:30
  146.1 1.8 %select_convert_fusion.1 = bf16[4,64,512]{2,1,0:T(8,128)(2,1)} fusion(bf16[4,64,512]{2,1,0:T(8,128)(2,1)} %reduce-scatter.8.cloned.1.call-done, pred[4,64]{1,0:T(4,128)(4,1)S(1)} %broadcast_compare_fusion.3), kind=kLoop, calls=%fused_computation.82 | loop fusion | flops 393216 | bytes 524544 | tf_op jit(solution)/shard_map/convert_element_type | solution.py:168
  147.8 9.1 %reduce-scatter.6.cloned.1.call-done = bf16[4,256,512]{2,1,0:T(8,128)(2,1)} async-done(((bf16[4,256,1024]{2,1,0:T(8,128)(2,1)}), bf16[4,256,512]{2,1,0:T(8,128)(2,1)}) %reduce-scatter.6.cloned.1.call-update) | async-done | bytes 1048592 | tf_op jit(solution)/shard_map/reduce_scatter | solution.py:162
  156.9 2.5 %fusion.31 = bf16[4,256,512]{2,1,0:T(8,128)(2,1)} fusion(bf16[4,256,512]{2,1,0:T(8,128)(2,1)S(1)} %get-tuple-element.6, bf16[4,256,512]{2,1,0:T(8,128)(2,1)} %reduce-scatter.6.cloned.1.call-done, pred[4,256]{1,0:T(4,128)(4,1)S(1)} %broadcast_compare_fusion.2), kind=kLoop, calls=%fused_computation.38 | loop fusion | flops 2621440 | bytes 3146752 | tf_op jit(solution)/shard_map/convert_element_type | solution.py:167
  (127 shorter events, 28.8 us)
Async XLA Ops:
  7.2 91.9 %copy-start = (bf16[512,1024]{1,0:T(8,128)(2,1)S(1)}, bf16[512,1024]{1,0:T(8,128)(2,1)}, u32[]{:S(2)}) copy-start(bf16[512,1024]{1,0:T(8,128)(2,1)} %param.22) | copy-start | bytes 3145732
  7.2 18.6 %all-gather.3.cloned.1.call-start = ((), (), s32[]{:S(2)}) async-start(), calls=%async_computation.3 | async-start | bytes 3145728 | tf_op jit(solution)/shard_map/all_gather | solution.py:73
  9.6 5.2 %copy-start.20 = (s32[4,64]{1,0:T(4,128)S(1)}, s32[4,64]{1,0:T(4,128)}, u32[]{:S(2)}) copy-start(s32[4,64]{1,0:T(4,128)} %param.15) | copy-start | bytes 3076
  12.3 101.6 %reduce-scatter.4.cloned.1.call-start = ((), (), s32[]{:S(2)}) async-start(), calls=%async_computation.4 | async-start | bytes 3145728 | tf_op jit(solution)/shard_map/reduce_scatter | solution.py:142
  14.7 11.1 %copy-start.3 = (bf16[4,64,1024]{2,1,0:T(8,128)(2,1)}, bf16[4,64,1024]{2,1,0:T(8,128)(2,1)S(1)}, u32[]{:S(2)}) copy-start(bf16[4,64,1024]{2,1,0:T(8,128)(2,1)S(1)} %all_gather.10) | copy-start | bytes 1572868
  30.6 9.0 %copy-start.1 = (bf16[4,256,1024]{2,1,0:T(8,128)(2,1)S(1)}, bf16[4,256,1024]{2,1,0:T(8,128)(2,1)}, u32[]{:S(2)}) copy-start(bf16[4,256,1024]{2,1,0:T(8,128)(2,1)} %all-gather.3.cloned.1.call-done) | copy-start | bytes 6291460
  43.8 17.1 %copy-start.7 = (bf16[4,320,512]{2,1,0:T(8,128)(2,1)}, bf16[4,320,512]{2,1,0:T(8,128)(2,1)S(1)}, u32[]{:S(2)}) copy-start(bf16[4,320,512]{2,1,0:T(8,128)(2,1)S(1)} %fusion.59) | copy-start | bytes 3932164
  45.4 15.6 %copy-start.6 = (bf16[4,320,512]{2,1,0:T(8,128)(2,1)}, bf16[4,320,512]{2,1,0:T(8,128)(2,1)S(1)}, u32[]{:S(2)}) copy-start(bf16[4,320,512]{2,1,0:T(8,128)(2,1)S(1)} %fusion.60) | copy-start | bytes 3932164
  45.4 12.9 %copy-start.25 = (bf16[1024,512]{1,0:T(8,128)(2,1)S(1)}, bf16[1024,512]{1,0:T(8,128)(2,1)}, u32[]{:S(2)}) copy-start(bf16[1024,512]{1,0:T(8,128)(2,1)} %param.19) | copy-start | bytes 3145732
  45.5 6.6 %copy-start.9 = (bf16[1,4,64,512]{3,2,1,0:T(8,128)(2,1)}, bf16[1,4,64,512]{3,2,1,0:T(8,128)(2,1)S(1)}, u32[]{:S(2)}) copy-start(bf16[1,4,64,512]{3,2,1,0:T(8,128)(2,1)S(1)} %get-tuple-element.22) | copy-start | bytes 786436
  45.5 7.5 %copy-start.11 = (bf16[1,4,64,512]{3,2,1,0:T(8,128)(2,1)}, bf16[1,4,64,512]{3,2,1,0:T(8,128)(2,1)S(1)}, u32[]{:S(2)}) copy-start(bf16[1,4,64,512]{3,2,1,0:T(8,128)(2,1)S(1)} %get-tuple-element.23) | copy-start | bytes 786436
  46.3 23.3 %collective-permute-start = (bf16[2,4,32,512]{3,2,1,0:T(8,128)(2,1)}, bf16[2,4,32,512]{3,2,1,0:T(8,128)(2,1)}, u32[]{:S(2)}, u32[]{:S(2)}) collective-permute-start(bf16[2,4,32,512]{3,2,1,0:T(8,128)(2,1)} %pad_maximum_fusion.8), channel_id=1, source_target_pairs={{0,2},{2,4},{4,6},{6,8},{8,10},{10,12},{12,14},{14,16},{16,18},{18... | collective-permute-start | bytes 786440 | tf_op jit(solution)/shard_map/ppermute | solution.py:18
  50.8 16.6 %collective-permute-start.1 = (bf16[2,4,4,512]{3,2,1,0:T(4,128)(2,1)S(1)}, bf16[2,4,4,512]{3,2,1,0:T(4,128)(2,1)S(1)}, u32[]{:S(2)}, u32[]{:S(2)}) collective-permute-start(bf16[2,4,4,512]{3,2,1,0:T(4,128)(2,1)S(1)} %pad_maximum_fusion.9), channel_id=1, source_target_pairs={{2,0},{4,2},{6,4},{8,6},{10,8},{12,10},{14,12},{16,14},{18,16},{20... | collective-permute-start | bytes 98312 | tf_op jit(solution)/shard_map/ppermute | solution.py:18
  52.9 19.7 %collective-permute-start.2 = (bf16[2,4,64,512]{3,2,1,0:T(8,128)(2,1)}, bf16[2,4,64,512]{3,2,1,0:T(8,128)(2,1)}, u32[]{:S(2)}, u32[]{:S(2)}) collective-permute-start(bf16[2,4,64,512]{3,2,1,0:T(8,128)(2,1)} %pad_maximum_fusion.7), channel_id=1, source_target_pairs={{0,2},{2,4},{4,6},{6,8},{8,10},{10,12},{12,14},{14,16},{16,18},{18... | collective-permute-start | bytes 1572872 | tf_op jit(solution)/shard_map/ppermute | solution.py:18
  66.0 6.6 %copy-start.10 = (bf16[1,4,64,512]{3,2,1,0:T(8,128)(2,1)S(1)}, bf16[1,4,64,512]{3,2,1,0:T(8,128)(2,1)}, u32[]{:S(2)}) copy-start(bf16[1,4,64,512]{3,2,1,0:T(8,128)(2,1)} %copy-done.9) | copy-start | bytes 786436
  66.0 6.6 %copy-start.12 = (bf16[1,4,64,512]{3,2,1,0:T(8,128)(2,1)S(1)}, bf16[1,4,64,512]{3,2,1,0:T(8,128)(2,1)}, u32[]{:S(2)}) copy-start(bf16[1,4,64,512]{3,2,1,0:T(8,128)(2,1)} %copy-done.11) | copy-start | bytes 786436
  75.1 13.0 %copy-start.13 = (bf16[4,256,512]{1,2,0:T(8,128)(2,1)S(1)}, bf16[4,256,512]{1,2,0:T(8,128)(2,1)}, u32[]{:S(2)}) copy-start(bf16[4,256,512]{1,2,0:T(8,128)(2,1)} %copy.27) | copy-start | bytes 3145732
  75.1 13.0 %copy-start.15 = (pred[4,320,420]{1,2,0:T(8,128)(4,1)S(1)}, pred[4,320,420]{1,2,0:T(8,128)(4,1)}, u32[]{:S(2)}) copy-start(pred[4,320,420]{1,2,0:T(8,128)(4,1)} %pad_add_fusion) | copy-start | bytes 1612804
  75.1 13.0 %copy-start.16 = (bf16[1,4,32,512]{2,3,1,0:T(8,128)(2,1)S(1)}, bf16[1,4,32,512]{2,3,1,0:T(8,128)(2,1)}, u32[]{:S(2)}) copy-start(bf16[1,4,32,512]{2,3,1,0:T(8,128)(2,1)} %copy.39) | copy-start | bytes 393220
  75.1 13.0 %copy-start.17 = (bf16[1,4,4,512]{2,3,1,0:T(8,128)(2,1)S(1)}, bf16[1,4,4,512]{2,3,1,0:T(8,128)(2,1)}, u32[]{:S(2)}) copy-start(bf16[1,4,4,512]{2,3,1,0:T(8,128)(2,1)} %copy.40) | copy-start | bytes 49156
  102.2 11.8 %copy-start.5 = (bf16[4,256,512]{2,1,0:T(8,128)(2,1)S(1)}, bf16[4,256,512]{2,1,0:T(8,128)(2,1)}, u32[]{:S(2)}) copy-start(bf16[4,256,512]{2,1,0:T(8,128)(2,1)} %select_convert_fusion) | copy-start | bytes 3145732
  103.7 27.9 %all-gather.5.cloned.1.call-start = ((), (), s32[]{:S(2)}) async-start(), calls=%async_computation.5 | async-start | bytes 3145728 | tf_op jit(solution)/shard_map/all_gather | solution.py:160
  119.6 26.4 %reduce-scatter.8.cloned.1.call-start = ((), (), s32[]{:S(2)}) async-start(), calls=%async_computation.7 | async-start | bytes 786432 | tf_op jit(solution)/shard_map/reduce_scatter | solution.py:145
  121.6 35.3 %reduce-scatter.6.cloned.1.call-start = ((), (), s32[]{:S(2)}) async-start(), calls=%async_computation.6 | async-start | bytes 3145728 | tf_op jit(solution)/shard_map/reduce_scatter | solution.py:162
  (12 other events, 26.7 us)
Sparse Core Ops, SparseCore 0:
  12.5 13.2 all-gather.2
  103.8 10.0 reduce-scatter.3
  119.7 11.8 all-gather.4
  133.7 9.0 reduce-scatter.7
  146.1 10.7 reduce-scatter.5
where the time goes:
time: 167 us; the launch traced here: 166 us
  matrix products  48.1 us (29%)
  waiting for transfers between devices  37.4 us (22%)
  local copies, waits for them, and re-layouts  26 us (16%)
  other arithmetic  23.9 us (14%)
  between operations  14.3 us (9%)
  starting transfers between devices  11.5 us (7%)
  blocking collectives  4.79 us (3%)
    dot_general x6, matrix products, product(): result = jnp.dot(flat_rows, weight, preferred_element_type=jnp.float32)  24.3 us
    dot_general x1, matrix products, body(): jnp.einsum('bqhd,bkhd->bhqk', query_heads, key_heads, preferred_element_t...  12.9 us
    ppermute x3, starting transfers between devices, from_behind(): return lax.ppermute(block, axis, route)  11.1 us
    dot_general x1, matrix products, body(): jnp.einsum('bhqk,bkhd->bqhd', shares, value_heads, preferred_element_type...  10.9 us
    all_gather x1, waiting for transfers between devices, body(): normed_ffn = lax.all_gather(normed_half, 'mp', axis=2, tiled=True)  9.98 us
    reduce_scatter x1, waiting for transfers between devices, body(): lax.psum_scatter(frame_term.astype(jnp.bfloat16), 'mp', scatter_dimension...  9.89 us
    reduce_scatter x1, waiting for transfers between devices, body(): lax.psum_scatter(rounded(product(hidden, w_down)).astype(jnp.bfloat16), '...  9.09 us
    all_gather x1, waiting for transfers between devices, body(): lax.all_gather(front_half, 'mp', axis=2, tiled=True)  8.35 us
  transfers between devices with their start and end apart: 8, of which 4 were waited for; matrix products, arithmetic and copies ran while one was open for 21% of the time, Pallas kernels for 0%

commit v1 on v0

--- a/solution.py
+++ b/solution.py
@@ -157,7 +157,8 @@
     normed_half = (
         (residual_f - center[..., None]) * lax.rsqrt(spread[..., None] + epsilon) * gain_half
     ).astype(jnp.bfloat16)
-    normed_ffn = lax.all_gather(normed_half, "mp", axis=2, tiled=True)
+    parts = lax.all_gather(normed_half, "mp")
+    normed_ffn = jnp.concatenate(parts, axis=2)
     hidden = jax.nn.gelu(product(normed_ffn, w_up)).astype(jnp.bfloat16)
     feed_half = lax.psum_scatter(
         rounded(product(hidden, w_down)).astype(jnp.bfloat16), "mp", scatter_dimension=2, tiled=True

time: 167 us -> 176 us (1.054)
  local copies, waits for them, and re-layouts: 26 us -> 35.5 us
    all_gather x0 -> x1, local copies, waits for them, and re-layouts: none -> 5.08 us  [body(): parts = lax.all_gather(normed_half, 'mp')]
    dot_general x1 -> x2, local copies, waits for them, and re-layouts: 0.67 us -> 5.11 us  [product(): result = jnp.dot(flat_rows, weight, preferred_element_type=jnp.float32)]
  transfers between devices with their start and end apart: 8 -> 8, of which waited for: 4 -> 4; matrix products, arithmetic and copies ran while one was open for 21% -> 25% of each run, Pallas kernels for 0% -> 0%
where the time goes in v1:
time: 176 us
  matrix products  48.2 us (27%)
  waiting for transfers between devices  37.4 us (21%)
  local copies, waits for them, and re-layouts  35.5 us (20%)
  other arithmetic  23.9 us (14%)
  between operations  14.3 us (8%)
  starting transfers between devices  11.5 us (7%)
  blocking collectives  4.79 us (3%)
    dot_general x6, matrix products, product(): result = jnp.dot(flat_rows, weight, preferred_element_type=jnp.float32)  24.4 us
    dot_general x1, matrix products, body(): jnp.einsum('bqhd,bkhd->bhqk', query_heads, key_heads, preferred_element_t...  12.9 us
    ppermute x3, starting transfers between devices, from_behind(): return lax.ppermute(block, axis, route)  11.1 us
    dot_general x1, matrix products, body(): jnp.einsum('bhqk,bkhd->bqhd', shares, value_heads, preferred_element_type...  10.9 us
    all_gather x1, waiting for transfers between devices, body(): parts = lax.all_gather(normed_half, 'mp')  9.98 us
    reduce_scatter x1, waiting for transfers between devices, body(): lax.psum_scatter(frame_term.astype(jnp.bfloat16), 'mp', scatter_dimension...  9.89 us
    reduce_scatter x1, waiting for transfers between devices, body(): lax.psum_scatter(rounded(product(hidden, w_down)).astype(jnp.bfloat16), '...  9.06 us
    all_gather x1, waiting for transfers between devices, body(): lax.all_gather(front_half, 'mp', axis=2, tiled=True)  8.35 us
  transfers between devices with their start and end apart: 8, of which 4 were waited for; matrix products, arithmetic and copies ran while one was open for 25% of the time, Pallas kernels for 0%

profile of v1, /device:TPU:0, one launch (start us, length us, event | category | flops | bytes accessed | tf_op | source)
XLA Modules:
  0.0 175.6 jit_solution(9814731270255909501)
XLA Ops:
  7.3 1.6 copy.39
  9.7 2.6 %select_convert_fusion = bf16[4,256,512]{2,1,0:T(8,128)(2,1)} fusion(bf16[4,256,320]{2,1,0:T(8,128)(2,1)S(1)} %dot_general.33, pred[4,256]{1,0:T(4,128)(4,1)S(1)} %broadcast_compare_fusion.2, bf16[320,512]{1,0:T(8,128)(2,1)} %param.17), kind=kOutput, calls=%fused_computation.56 | convolution fusion | flops 336592896 | bytes 2032640 | tf_op jit(solution)/shard_map/dot_general | solution.py:30
  12.4 2.3 %all_gather.13 = bf16[4,64,1024]{2,1,0:T(8,128)(2,1)S(1)} all-gather(bf16[4,64,512]{2,1,0:T(8,128)(2,1)S(1)} %copy-done.18), channel_id=1, replica_groups=mesh['tm'=16,'mp'=2] {'mp'}, dimensions={2}, use_global_device_ids=true | all-gather | bytes 786432 | tf_op jit(solution)/shard_map/all_gather | solution.py:74
  17.5 8.4 %all-gather.4.cloned.1.call-done = bf16[4,256,1024]{2,1,0:T(8,128)(2,1)} async-done(((bf16[4,256,512]{2,1,0:T(8,128)(2,1)}), bf16[4,256,1024]{2,1,0:T(8,128)(2,1)}) %all-gather.4.cloned.1.call-update) | async-done | bytes 2097168 | tf_op jit(solution)/shard_map/all_gather | solution.py:73
  25.8 4.8 %reshape.354 = f32[4,64,4,1024]{3,2,1,0:T(4,128)} reshape(bf16[4,256,1024]{2,1,0:T(8,128)(2,1)} %all-gather.4.cloned.1.call-done) | data formatting | bytes 6291456 | tf_op jit(solution)/shard_map/reshape | solution.py:77
  30.6 5.9 %reduce_sum.94 = f32[4,64,1024]{2,1,0:T(8,128)} reduce(f32[4,64,4,1024]{3,2,1,0:T(4,128)} %reshape.354, f32[]{:T(128)} %constant.29.clone.1), dimensions={2}, to_apply=%region_4.5 | reduce | flops 786432 | bytes 5242884 | tf_op jit(solution)/shard_map/reduce_sum | solution.py:77
  37.9 1.6 multiply_reduce_fusion.1
  46.3 4.5 %collective-permute-start = (bf16[2,4,32,512]{3,2,1,0:T(8,128)(2,1)}, bf16[2,4,32,512]{3,2,1,0:T(8,128)(2,1)}, u32[]{:S(2)}, u32[]{:S(2)}) collective-permute-start(bf16[2,4,32,512]{3,2,1,0:T(8,128)(2,1)} %pad_maximum_fusion.8), channel_id=1, source_target_pairs={{0,2},{2,4},{4,6},{6,8},{8,10},{10,12},{12,14},{14,16},{16,18},{18... | collective-permute-start | bytes 786440 | tf_op jit(solution)/shard_map/ppermute | solution.py:18
  52.9 5.3 %collective-permute-start.2 = (bf16[2,4,64,512]{3,2,1,0:T(8,128)(2,1)}, bf16[2,4,64,512]{3,2,1,0:T(8,128)(2,1)}, u32[]{:S(2)}, u32[]{:S(2)}) collective-permute-start(bf16[2,4,64,512]{3,2,1,0:T(8,128)(2,1)} %pad_maximum_fusion.7), channel_id=1, source_target_pairs={{0,2},{2,4},{4,6},{6,8},{8,10},{10,12},{12,14},{14,16},{16,18},{18... | collective-permute-start | bytes 1572872 | tf_op jit(solution)/shard_map/ppermute | solution.py:18
  58.3 2.6 %fusion.61 = bf16[4,320,512]{2,1,0:T(8,128)(2,1)} fusion(bf16[4,64,1024]{2,1,0:T(8,128)(2,1)S(1)} %get-tuple-element.16, bf16[4,256,1024]{2,1,0:T(8,128)(2,1)S(1)} %multiply_convert_fusion, bf16[1024,512]{1,0:T(8,128)(2,1)S(1)} %copy-done.25), kind=kOutput, calls=%fused_computation.64 | convolution fusion | flops 1348075520 | bytes 4980736 | tf_op jit(solution)/shard_map/dot_general | solution.py:30
  63.4 2.6 %copy.45 = bf16[4,320,512]{1,2,0:T(8,128)(2,1)} copy(bf16[4,320,512]{2,1,0:T(8,128)(2,1)} %fusion.61) | data formatting | bytes 2621440 | tf_op jit(solution)/shard_map/convert_element_type | solution.py:86
  75.2 12.9 %fusion = (f32[4,8,320]{2,1,0:T(8,128)S(1)}, f32[4,8,320,420]{2,3,1,0:T(8,128)}) fusion(pred[4,320,420]{1,2,0:T(8,128)(4,1)} %pad_add_fusion, bf16[4,320,8,64]{1,3,2,0:T(8,128)(2,1)} %bitcast.63, bf16[4,128,8,64]{1,3,2,0:T(8,128)(2,1)} %bitcast.71, bf16[4,4,8,64]{1,3,2,0:T(8,128)(2,1)} %bitcast.69, bf16[4,256,8,64]{1,3,2,0:T(8,128)(2,1)S(1)} %bitcast.65, ...), kind=kOutput, calls=%fused_computation.2 | convolution fusion | flops 570275840 | bytes 20812800 | tf_op jit(solution)/shard_map/bqhd,bkhd->bhqk/dot_general | solution.py:131
  88.1 10.9 %fusion.54 = bf16[4,8,64,320]{3,2,1,0:T(8,128)(2,1)S(1)} fusion(f32[4,8,320,420]{2,3,1,0:T(8,128)} %get-tuple-element.21, f32[4,8,320]{2,1,0:T(8,128)S(1)} %get-tuple-element.20, pred[4,320,420]{1,2,0:T(8,128)(4,1)S(1)} %copy-done.15, bf16[4,128,8,64]{1,3,2,0:T(8,128)(2,1)S(1)} %bitcast.70, bf16[4,4,8,64]{1,3,2,0:T(8,128)(2,1)S(1)} %bitcast.68, ...), kind=kOutput, calls=%fused_computation.59 | convolution fusion | flops 575242240 | bytes 20812800 | tf_op jit(solution)/shard_map/bhqk,bkhd->bqhd/dot_general | solution.py:136
  104.0 9.9 %reduce-scatter.4.cloned.1.call-done = bf16[4,256,512]{2,1,0:T(8,128)(2,1)} async-done(((bf16[4,256,1024]{2,1,0:T(8,128)(2,1)}), bf16[4,256,512]{2,1,0:T(8,128)(2,1)}) %reduce-scatter.4.cloned.1.call-update) | async-done | bytes 1048592 | tf_op jit(solution)/shard_map/reduce_scatter | solution.py:142
  113.9 1.8 convert_reduce_fusion
  115.7 2.5 %all-reduce = (f32[4,256]{1,0:T(4,128)S(1)}, f32[4,256]{1,0:T(4,128)S(1)}) all-reduce(f32[4,256]{1,0:T(4,128)S(1)} %get-tuple-element.3, f32[4,256]{1,0:T(4,128)S(1)} %get-tuple-element.2), channel_id=1, replica_groups=mesh['tm'=16,'mp'=2] {'mp'}, use_global_device_ids=true, to_apply=%region_12.13 | all-reduce | flops 2048 | bytes 16384 | tf_op jit(solution)/shard_map/psum | solution.py:151
  119.7 1.9 %slice.95 = bf16[4,64,1024]{2,1,0:T(8,128)(2,1)} slice(bf16[4,320,1024]{2,1,0:T(8,128)(2,1)} %copy-done.8), slice={[0:4], [256:320], [0:1024]} | slice | bytes 1048576 | tf_op jit(solution)/shard_map/slice | solution.py:140
  121.6 10.0 %all-gather.6.cloned.1.call-done = bf16[8,256,512]{2,1,0:T(8,128)(2,1)} async-done(((bf16[4,256,512]{2,1,0:T(8,128)(2,1)}), bf16[8,256,512]{2,1,0:T(8,128)(2,1)}) %all-gather.6.cloned.1.call-update) | async-done | bytes 2097168 | tf_op jit(solution)/shard_map/all_gather | solution.py:160
  131.6 5.1 %copy.59 = bf16[2,4,256,512]{3,0,2,1:T(2,128)(2,1)} copy(bf16[2,4,256,512]{3,2,1,0:T(8,128)(2,1)} %bitcast.62) | data formatting | bytes 4194304 | tf_op jit(solution)/shard_map/all_gather | solution.py:160
  136.7 4.4 %dot_general.42 = bf16[4,256,1024]{2,1,0:T(8,128)(2,1)} reshape(bf16[4,256,2,512]{3,2,1,0:T(2,128)(2,1)} %bitcast.61) | data formatting | bytes 4194304 | tf_op jit(solution)/shard_map/dot_general | solution.py:30
  141.1 14.4 %fusion.47 = bf16[4,256,1024]{2,1,0:T(8,128)(2,1)} fusion(bf16[2048,1024]{1,0:T(8,128)(2,1)} %param.25, bf16[4,256,1024]{2,1,0:T(8,128)(2,1)} %dot_general.42, bf16[1024,2048]{1,0:T(8,128)(2,1)} %param.24), kind=kOutput, calls=%fused_computation.58 | convolution fusion | flops 8609857536 | bytes 12582912 | tf_op jit(solution)/shard_map/dot_general | solution.py:30
  155.7 1.8 %select_convert_fusion.1 = bf16[4,64,512]{2,1,0:T(8,128)(2,1)} fusion(bf16[4,64,512]{2,1,0:T(8,128)(2,1)} %reduce-scatter.8.cloned.1.call-done, pred[4,64]{1,0:T(4,128)(4,1)S(1)} %broadcast_compare_fusion.3), kind=kLoop, calls=%fused_computation.83 | loop fusion | flops 393216 | bytes 524544 | tf_op jit(solution)/shard_map/convert_element_type | solution.py:169
  157.5 9.1 %reduce-scatter.6.cloned.1.call-done = bf16[4,256,512]{2,1,0:T(8,128)(2,1)} async-done(((bf16[4,256,1024]{2,1,0:T(8,128)(2,1)}), bf16[4,256,512]{2,1,0:T(8,128)(2,1)}) %reduce-scatter.6.cloned.1.call-update) | async-done | bytes 1048592 | tf_op jit(solution)/shard_map/reduce_scatter | solution.py:163
  166.5 2.5 %fusion.31 = bf16[4,256,512]{2,1,0:T(8,128)(2,1)} fusion(bf16[4,256,512]{2,1,0:T(8,128)(2,1)S(1)} %get-tuple-element.6, bf16[4,256,512]{2,1,0:T(8,128)(2,1)} %reduce-scatter.6.cloned.1.call-done, pred[4,256]{1,0:T(4,128)(4,1)S(1)} %broadcast_compare_fusion.2), kind=kLoop, calls=%fused_computation.38 | loop fusion | flops 2621440 | bytes 3146752 | tf_op jit(solution)/shard_map/convert_element_type | solution.py:168
  (129 shorter events, 31.9 us)
Async XLA Ops:
  7.2 91.9 %copy-start = (bf16[512,1024]{1,0:T(8,128)(2,1)S(1)}, bf16[512,1024]{1,0:T(8,128)(2,1)}, u32[]{:S(2)}) copy-start(bf16[512,1024]{1,0:T(8,128)(2,1)} %param.22) | copy-start | bytes 3145732
  7.2 18.6 %all-gather.4.cloned.1.call-start = ((), (), s32[]{:S(2)}) async-start(), calls=%async_computation.3 | async-start | bytes 3145728 | tf_op jit(solution)/shard_map/all_gather | solution.py:73
  9.6 5.2 %copy-start.20 = (s32[4,64]{1,0:T(4,128)S(1)}, s32[4,64]{1,0:T(4,128)}, u32[]{:S(2)}) copy-start(s32[4,64]{1,0:T(4,128)} %param.15) | copy-start | bytes 3076
  12.3 101.6 %reduce-scatter.4.cloned.1.call-start = ((), (), s32[]{:S(2)}) async-start(), calls=%async_computation.4 | async-start | bytes 3145728 | tf_op jit(solution)/shard_map/reduce_scatter | solution.py:142
  14.7 11.1 %copy-start.3 = (bf16[4,64,1024]{2,1,0:T(8,128)(2,1)}, bf16[4,64,1024]{2,1,0:T(8,128)(2,1)S(1)}, u32[]{:S(2)}) copy-start(bf16[4,64,1024]{2,1,0:T(8,128)(2,1)S(1)} %all_gather.13) | copy-start | bytes 1572868
  30.6 9.0 %copy-start.1 = (bf16[4,256,1024]{2,1,0:T(8,128)(2,1)S(1)}, bf16[4,256,1024]{2,1,0:T(8,128)(2,1)}, u32[]{:S(2)}) copy-start(bf16[4,256,1024]{2,1,0:T(8,128)(2,1)} %all-gather.4.cloned.1.call-done) | copy-start | bytes 6291460
  43.8 17.1 %copy-start.7 = (bf16[4,320,512]{2,1,0:T(8,128)(2,1)}, bf16[4,320,512]{2,1,0:T(8,128)(2,1)S(1)}, u32[]{:S(2)}) copy-start(bf16[4,320,512]{2,1,0:T(8,128)(2,1)S(1)} %fusion.59) | copy-start | bytes 3932164
  45.4 15.6 %copy-start.6 = (bf16[4,320,512]{2,1,0:T(8,128)(2,1)}, bf16[4,320,512]{2,1,0:T(8,128)(2,1)S(1)}, u32[]{:S(2)}) copy-start(bf16[4,320,512]{2,1,0:T(8,128)(2,1)S(1)} %fusion.60) | copy-start | bytes 3932164
  45.4 12.9 %copy-start.25 = (bf16[1024,512]{1,0:T(8,128)(2,1)S(1)}, bf16[1024,512]{1,0:T(8,128)(2,1)}, u32[]{:S(2)}) copy-start(bf16[1024,512]{1,0:T(8,128)(2,1)} %param.19) | copy-start | bytes 3145732
  45.5 6.6 %copy-start.9 = (bf16[1,4,64,512]{3,2,1,0:T(8,128)(2,1)}, bf16[1,4,64,512]{3,2,1,0:T(8,128)(2,1)S(1)}, u32[]{:S(2)}) copy-start(bf16[1,4,64,512]{3,2,1,0:T(8,128)(2,1)S(1)} %get-tuple-element.22) | copy-start | bytes 786436
  45.5 7.5 %copy-start.11 = (bf16[1,4,64,512]{3,2,1,0:T(8,128)(2,1)}, bf16[1,4,64,512]{3,2,1,0:T(8,128)(2,1)S(1)}, u32[]{:S(2)}) copy-start(bf16[1,4,64,512]{3,2,1,0:T(8,128)(2,1)S(1)} %get-tuple-element.23) | copy-start | bytes 786436
  46.3 23.3 %collective-permute-start = (bf16[2,4,32,512]{3,2,1,0:T(8,128)(2,1)}, bf16[2,4,32,512]{3,2,1,0:T(8,128)(2,1)}, u32[]{:S(2)}, u32[]{:S(2)}) collective-permute-start(bf16[2,4,32,512]{3,2,1,0:T(8,128)(2,1)} %pad_maximum_fusion.8), channel_id=1, source_target_pairs={{0,2},{2,4},{4,6},{6,8},{8,10},{10,12},{12,14},{14,16},{16,18},{18... | collective-permute-start | bytes 786440 | tf_op jit(solution)/shard_map/ppermute | solution.py:18
  50.8 16.6 %collective-permute-start.1 = (bf16[2,4,4,512]{3,2,1,0:T(4,128)(2,1)S(1)}, bf16[2,4,4,512]{3,2,1,0:T(4,128)(2,1)S(1)}, u32[]{:S(2)}, u32[]{:S(2)}) collective-permute-start(bf16[2,4,4,512]{3,2,1,0:T(4,128)(2,1)S(1)} %pad_maximum_fusion.9), channel_id=1, source_target_pairs={{2,0},{4,2},{6,4},{8,6},{10,8},{12,10},{14,12},{16,14},{18,16},{20... | collective-permute-start | bytes 98312 | tf_op jit(solution)/shard_map/ppermute | solution.py:18
  52.9 19.7 %collective-permute-start.2 = (bf16[2,4,64,512]{3,2,1,0:T(8,128)(2,1)}, bf16[2,4,64,512]{3,2,1,0:T(8,128)(2,1)}, u32[]{:S(2)}, u32[]{:S(2)}) collective-permute-start(bf16[2,4,64,512]{3,2,1,0:T(8,128)(2,1)} %pad_maximum_fusion.7), channel_id=1, source_target_pairs={{0,2},{2,4},{4,6},{6,8},{8,10},{10,12},{12,14},{14,16},{16,18},{18... | collective-permute-start | bytes 1572872 | tf_op jit(solution)/shard_map/ppermute | solution.py:18
  66.0 6.6 %copy-start.10 = (bf16[1,4,64,512]{3,2,1,0:T(8,128)(2,1)S(1)}, bf16[1,4,64,512]{3,2,1,0:T(8,128)(2,1)}, u32[]{:S(2)}) copy-start(bf16[1,4,64,512]{3,2,1,0:T(8,128)(2,1)} %copy-done.9) | copy-start | bytes 786436
  66.0 6.6 %copy-start.12 = (bf16[1,4,64,512]{3,2,1,0:T(8,128)(2,1)S(1)}, bf16[1,4,64,512]{3,2,1,0:T(8,128)(2,1)}, u32[]{:S(2)}) copy-start(bf16[1,4,64,512]{3,2,1,0:T(8,128)(2,1)} %copy-done.11) | copy-start | bytes 786436
  75.1 13.0 %copy-start.13 = (bf16[4,256,512]{1,2,0:T(8,128)(2,1)S(1)}, bf16[4,256,512]{1,2,0:T(8,128)(2,1)}, u32[]{:S(2)}) copy-start(bf16[4,256,512]{1,2,0:T(8,128)(2,1)} %copy.41) | copy-start | bytes 3145732
  75.1 13.0 %copy-start.15 = (pred[4,320,420]{1,2,0:T(8,128)(4,1)S(1)}, pred[4,320,420]{1,2,0:T(8,128)(4,1)}, u32[]{:S(2)}) copy-start(pred[4,320,420]{1,2,0:T(8,128)(4,1)} %pad_add_fusion) | copy-start | bytes 1612804
  75.1 13.0 %copy-start.16 = (bf16[1,4,32,512]{2,3,1,0:T(8,128)(2,1)S(1)}, bf16[1,4,32,512]{2,3,1,0:T(8,128)(2,1)}, u32[]{:S(2)}) copy-start(bf16[1,4,32,512]{2,3,1,0:T(8,128)(2,1)} %copy.54) | copy-start | bytes 393220
  75.1 13.0 %copy-start.17 = (bf16[1,4,4,512]{2,3,1,0:T(8,128)(2,1)S(1)}, bf16[1,4,4,512]{2,3,1,0:T(8,128)(2,1)}, u32[]{:S(2)}) copy-start(bf16[1,4,4,512]{2,3,1,0:T(8,128)(2,1)} %copy.55) | copy-start | bytes 49156
  102.2 11.8 %copy-start.5 = (bf16[4,256,512]{2,1,0:T(8,128)(2,1)S(1)}, bf16[4,256,512]{2,1,0:T(8,128)(2,1)}, u32[]{:S(2)}) copy-start(bf16[4,256,512]{2,1,0:T(8,128)(2,1)} %select_convert_fusion) | copy-start | bytes 3145732
  103.7 27.9 %all-gather.6.cloned.1.call-start = ((), (), s32[]{:S(2)}) async-start(), calls=%async_computation.7 | async-start | bytes 3145728 | tf_op jit(solution)/shard_map/all_gather | solution.py:160
  119.6 36.1 %reduce-scatter.8.cloned.1.call-start = ((), (), s32[]{:S(2)}) async-start(), calls=%async_computation.6 | async-start | bytes 786432 | tf_op jit(solution)/shard_map/reduce_scatter | solution.py:145
  121.6 45.0 %reduce-scatter.6.cloned.1.call-start = ((), (), s32[]{:S(2)}) async-start(), calls=%async_computation.5 | async-start | bytes 3145728 | tf_op jit(solution)/shard_map/reduce_scatter | solution.py:163
  (12 other events, 26.7 us)
Sparse Core Ops, SparseCore 0:
  12.5 13.2 all-gather.3
  103.8 10.0 reduce-scatter.3
  119.7 11.8 all-gather.5
  133.7 9.0 reduce-scatter.7
  155.7 10.7 reduce-scatter.5
